TPU v7x, 32 devices: a whole 2x2x4 slice. The times are simulated.
32 devices in a mesh: grp: 4 (over x, core), dp: 8 (over z, y).
Axes of the slice: x: 2, y: 2, z: 4, core: 2. Of those that a mesh axis runs over, the one named last changes fastest.
Arguments:
- query: bfloat16 [8, 512, 2560], P('dp', 'grp'), may hold values from -30 to 30
- resp_kv: bfloat16 [8, 512, 1024], P('dp', 'grp'), may hold values from -6 to 6
- prefix_kv: bfloat16 [8, 64, 1024], P('dp', 'grp'), may hold values from -30 to 30
- query_bias: float32 [2560], replicated, may hold values from -3 to 3
- kv_bias: float32 [1024], replicated, may hold values from -3 to 3
- out_grad: bfloat16 [8, 512, 2560], P('dp', 'grp'), may hold values from -6 to 6
- lengths: int32 [8, 4], P('dp', 'grp'), may hold values from 32 to 128
Outputs:
- attended: bfloat16 [8, 512, 2560], P('dp', 'grp')
- query_grad: bfloat16 [8, 512, 2560], P('dp', 'grp')
- resp_kv_grad: bfloat16 [8, 512, 1024], P('dp', 'grp')
- prefix_kv_grad: bfloat16 [8, 64, 1024], P('dp', 'grp')
- query_bias_grad: float32 [2560], replicated
- kv_bias_grad: float32 [1024], replicated
All inputs are finite; a program needn't handle non-finite values.
Results may differ from a plain program's by a relative error of at most 0.013.
The roundings to bfloat16 on the way count: a program that leaves them out, or rounds other values in their place, can miss the bound.
Values may be sent and summed in bfloat16 or wider, within the bound.
A program may use at most 64 MiB of HBM per device.

v0:
```python
import jax
import jax.numpy as jnp
from jax import lax
from jax.sharding import PartitionSpec as P

QH = 20
KVH = 4
HD = 128


NEG_BIG = -1e30


def attend_group(queries, cotangent, key_blocks, value_blocks, allows):
    factor = queries.shape[-1] ** (-0.5)
    scores = []
    for keys, allow in zip(key_blocks, allows):
        raw = jnp.einsum("thd,sd->hts", queries, keys, preferred_element_type=jnp.float32) * factor
        scores.append(jnp.where(allow[None], raw, NEG_BIG))
    highest = jnp.max(scores[0], -1, keepdims=True)
    for item in scores[1:]:
        highest = jnp.maximum(highest, jnp.max(item, -1, keepdims=True))
    powers = [jnp.exp(item - highest) for item in scores]
    totals = sum((jnp.sum(item, -1, keepdims=True) for item in powers))
    chances = [item / totals for item in powers]
    rounded = [item.astype(jnp.bfloat16) for item in chances]
    output = sum(
        (
            jnp.einsum("hts,sd->thd", wts, vals, preferred_element_type=jnp.float32)
            for wts, vals in zip(rounded, value_blocks)
        )
    )
    slopes = [
        jnp.einsum("thd,sd->hts", cotangent, vals, preferred_element_type=jnp.float32)
        for vals in value_blocks
    ]
    row_dot = sum(
        (jnp.sum(prob * slope, -1, keepdims=True) for prob, slope in zip(chances, slopes))
    )
    shifted = [
        (prob * (slope - row_dot)).astype(jnp.bfloat16) for prob, slope in zip(chances, slopes)
    ]
    query_grad = (
        sum(
            (
                jnp.einsum("hts,sd->thd", dsb, keys, preferred_element_type=jnp.float32)
                for dsb, keys in zip(shifted, key_blocks)
            )
        )
        * factor
    )
    key_grads = [
        jnp.einsum("hts,thd->sd", dsb, queries, preferred_element_type=jnp.float32) * factor
        for dsb in shifted
    ]
    value_grads = [
        jnp.einsum("hts,thd->sd", wts, cotangent, preferred_element_type=jnp.float32)
        for wts in rounded
    ]
    return (output, query_grad, key_grads, value_grads, shifted, rounded)


def local(query, resp_kv, prefix_kv, query_bias, kv_bias, out_grad, lengths):
    group = QH // KVH
    width = KVH * HD
    factor = HD ** (-0.5)
    prefix_own = (prefix_kv[0].astype(jnp.float32) + kv_bias).astype(jnp.bfloat16)
    own_rows = prefix_own.shape[0]
    prefix = lax.all_gather(prefix_own, "grp", axis=0, tiled=True)
    slots = query.shape[1]
    pre_rows = prefix.shape[0]
    length = lengths[0, 0]
    biased_query = (query[0].astype(jnp.float32) + query_bias).astype(jnp.bfloat16)
    own_kv = (resp_kv[0].astype(jnp.float32) + kv_bias).astype(jnp.bfloat16)
    position = jnp.arange(slots, dtype=jnp.int32)
    live = position < length
    grad_live = jnp.where(live[:, None], out_grad[0], jnp.zeros_like(out_grad[0]))
    allow_own = position[None, :] <= position[:, None]
    allow_pre = jnp.ones((slots, pre_rows), dtype=bool)
    queries = biased_query.reshape(slots, KVH, group, HD).transpose(1, 0, 2, 3)
    grads = grad_live.reshape(slots, KVH, group, HD).transpose(1, 0, 2, 3)
    pre_keys = prefix[:, :width].reshape(pre_rows, KVH, HD).transpose(1, 0, 2)
    pre_vals = prefix[:, width:].reshape(pre_rows, KVH, HD).transpose(1, 0, 2)
    own_keys = own_kv[:, :width].reshape(slots, KVH, HD).transpose(1, 0, 2)
    own_vals = own_kv[:, width:].reshape(slots, KVH, HD).transpose(1, 0, 2)

    def per_group(pieces):
        qpart, gpart, pkey, pval, okey, oval = pieces
        output, qgrad, kgrads, vgrads, shifted, rounded = attend_group(
            qpart,
            gpart,
            [jnp.concatenate([pkey, okey], 0)],
            [jnp.concatenate([pval, oval], 0)],
            [jnp.concatenate([allow_pre, allow_own], 1)],
        )
        return (
            output,
            qgrad,
            kgrads[0][:pre_rows],
            vgrads[0][:pre_rows],
            kgrads[0][pre_rows:],
            vgrads[0][pre_rows:],
            shifted[0][:, :, :pre_rows],
            rounded[0][:, :, :pre_rows],
        )

    output, qgrad, pk_grad, pv_grad, ok_grad, ov_grad, pre_shift, pre_prob = lax.map(
        per_group, (queries, grads, pre_keys, pre_vals, own_keys, own_vals)
    )
    output = output.transpose(1, 0, 2, 3).reshape(slots, QH * HD)
    attended = jnp.where(live[:, None], output, 0.0).astype(jnp.bfloat16)
    qgrad = qgrad.transpose(1, 0, 2, 3).reshape(slots, QH * HD)
    own_grad = jnp.concatenate(
        [
            ok_grad.transpose(1, 0, 2).reshape(slots, width),
            ov_grad.transpose(1, 0, 2).reshape(slots, width),
        ],
        -1,
    )
    shift_sum = jnp.sum(pre_shift.astype(jnp.float32), -1)
    prob_sum = jnp.sum(pre_prob.astype(jnp.float32), -1)
    key_total = jnp.einsum("jht,jthd->jd", shift_sum, queries.astype(jnp.float32)) * factor
    value_total = jnp.einsum("jht,jthd->jd", prob_sum, grads.astype(jnp.float32))
    pre_total = jnp.concatenate([key_total.reshape(width), value_total.reshape(width)], -1)
    count = lax.axis_size("grp") * own_rows
    shift_part = lax.slice_in_dim(pre_shift, 0, count, axis=3)
    prob_part = lax.slice_in_dim(pre_prob, 0, count, axis=3)
    key_part = (
        jnp.einsum("jhts,jthd->sjd", shift_part, queries, preferred_element_type=jnp.float32)
        * factor
    )
    value_part = jnp.einsum("jhts,jthd->sjd", prob_part, grads, preferred_element_type=jnp.float32)
    prefix_grad = lax.psum_scatter(
        jnp.concatenate(
            [key_part.reshape(count, width), value_part.reshape(count, width)], -1
        ).astype(jnp.bfloat16),
        "grp",
        scatter_dimension=0,
        tiled=True,
    )
    qsum, kvsum = lax.psum((jnp.sum(qgrad, 0), jnp.sum(own_grad, 0) + pre_total), ("grp", "dp"))
    return (
        attended[None],
        qgrad.astype(jnp.bfloat16)[None],
        own_grad.astype(jnp.bfloat16)[None],
        prefix_grad[None],
        qsum,
        kvsum,
    )


def solution(mesh):
    return jax.shard_map(
        local,
        mesh=mesh,
        in_specs=(
            P("dp", "grp", None),
            P("dp", "grp", None),
            P("dp", "grp", None),
            P(),
            P(),
            P("dp", "grp", None),
            P("dp", "grp"),
        ),
        out_specs=(
            P("dp", "grp", None),
            P("dp", "grp", None),
            P("dp", "grp", None),
            P("dp", "grp", None),
            P(),
            P(),
        ),
        check_vma=False,
    )
```

profile of v0, /device:TPU:0, one launch (start us, length us, event | category | flops | bytes accessed | tf_op | source)
XLA Modules:
  0.0 98.3 jit_solution(17740030026731421601)
XLA Ops:
  8.0 0.8 add.43
  8.7 0.8 fusion.49
  9.5 6.5 %all_gather.3 = bf16[64,1024]{1,0:T(8,128)(2,1)S(1)} all-gather(bf16[16,1024]{1,0:T(8,128)(2,1)S(1)} %fusion.49), channel_id=1, replica_groups=mesh['grp'=4,'dp'=8] {'grp'}, dimensions={0}, use_global_device_ids=true | all-gather | bytes 163840 | tf_op jit(solution)/shard_map/all_gather | solution.py:69
  16.7 1.1 %copy.17 = bf16[1,128,1024]{1,2,0:T(8,128)(2,1)S(1)} copy(bf16[1,128,1024]{2,1,0:T(8,128)(2,1)} %param.10) | data formatting | bytes 524288 | tf_op args[1]
  20.0 22.9 %while.21 = (s32[]{:T(128)}, bf16[4,128,5,128]{1,3,2,0:T(8,128)(2,1)}, f32[4,128,5,128]{1,3,2,0:T(8,128)}, f32[4,128,128]{1,2,0:T(8,128)}, f32[4,128,128]{1,2,0:...) while((s32[]{:T(128)}, ...), condition=%wide.region_4.5_spmd.clone, body=%wide.region_0.4_spmd.clone.sunk | while | flops 190725696 | bytes 7174342 | solution.py:107
  20.0 0.7 dynamic-slice_bitcast_fusion.5
  20.9 0.8 constant_dynamic-slice_fusion.5
  23.9 0.9 fusion.89
  24.8 1.0 fusion.90
  25.7 0.7 dynamic-slice_bitcast_fusion.5
  26.6 0.8 constant_dynamic-slice_fusion.5
  29.6 0.9 fusion.89
  30.5 1.0 fusion.90
  32.3 0.8 constant_dynamic-slice_fusion.5
  35.3 0.9 fusion.89
  36.2 1.0 fusion.90
  38.1 0.8 constant_dynamic-slice_fusion.5
  41.0 0.9 fusion.89
  41.9 1.0 fusion.90
  45.0 0.8 copy-done.2
  46.3 1.1 %copy.34 = bf16[1,128,2560]{2,1,0:T(8,128)(2,1)} copy(bf16[1,128,2560]{1,2,0:T(8,128)(2,1)S(1)} %select_convert_fusion) | data formatting | bytes 1310720
  47.4 1.1 %copy.35 = bf16[1,128,2560]{2,1,0:T(8,128)(2,1)} copy(bf16[1,128,2560]{1,2,0:T(8,128)(2,1)S(1)} %bitcast.229) | data formatting | bytes 1310720
  49.7 41.1 %all-reduce.1 = (f32[2560]{0:T(1024)}, f32[1024]{0:T(1024)}) all-reduce(f32[2560]{0:T(1024)S(1)} %reduce_sum.57, f32[1024]{0:T(1024)S(1)} %maximum_add_fusion), channel_id=1, replica_groups=mesh['grp'=4,'dp'=8] {'grp','dp'}, use_global_device_ids=true, to_apply=%region_7.8 | all-reduce | flops 3584 | bytes 28672 | tf_op jit(solution)/shard_map/psum | solution.py:141
  90.7 0.7 pad_maximum_fusion
  (132 shorter events, 17.0 us)
Async XLA Ops:
  7.2 10.7 %copy-start.9 = (f32[1024]{0:T(1024)S(1)}, f32[1024]{0:T(1024)}, u32[]{:S(2)}) copy-start(f32[1024]{0:T(1024)} %param.13) | copy-start | bytes 12292
  7.2 84.3 %reduce-scatter.2.cloned.1.call-start = ((), (), s32[]{:S(2)}) async-start(), calls=%async_computation.1 | async-start | bytes 163840 | tf_op jit(solution)/shard_map/reduce_scatter | solution.py:133
  7.9 12.0 %copy-start.10 = (pred[128]{0:T(512)(128)(4,1)}, pred[128]{0:T(512)(128)(4,1)S(1)}, u32[]{:S(2)}) copy-start(pred[128]{0:T(512)(128)(4,1)S(1)} %iota_compare_fusion.1) | copy-start | bytes 388
  8.0 10.8 %copy-start.6 = (bf16[1,128,2560]{2,1,0:T(8,128)(2,1)S(1)}, bf16[1,128,2560]{2,1,0:T(8,128)(2,1)}, u32[]{:S(2)}) copy-start(bf16[1,128,2560]{2,1,0:T(8,128)(2,1)} %param.9) | copy-start | bytes 1966084
  18.1 1.1 %copy-start.7 = (bf16[1,128,2560]{2,1,0:T(8,128)(2,1)S(1)}, bf16[1,128,2560]{2,1,0:T(8,128)(2,1)}, u32[]{:S(2)}) copy-start(bf16[1,128,2560]{2,1,0:T(8,128)(2,1)} %param.14) | copy-start | bytes 1966084
  42.9 1.5 %copy-start.1 = (bf16[4,5,128,64]{2,3,1,0:T(8,128)(2,1)}, bf16[4,5,128,64]{2,3,1,0:T(8,128)(2,1)S(1)}, u32[]{:S(2)}) copy-start(bf16[4,5,128,64]{2,3,1,0:T(8,128)(2,1)S(1)} %get-tuple-element.88) | copy-start | bytes 983044
  42.9 1.5 %copy-start.3 = (bf16[4,5,128,64]{2,3,1,0:T(8,128)(2,1)}, bf16[4,5,128,64]{2,3,1,0:T(8,128)(2,1)S(1)}, u32[]{:S(2)}) copy-start(bf16[4,5,128,64]{2,3,1,0:T(8,128)(2,1)S(1)} %get-tuple-element.87) | copy-start | bytes 983044
  42.9 1.6 %copy-start = (f32[4,128,5,128]{1,3,2,0:T(8,128)S(1)}, f32[4,128,5,128]{1,3,2,0:T(8,128)}, u32[]{:S(2)}) copy-start(f32[4,128,5,128]{1,3,2,0:T(8,128)} %get-tuple-element.84) | copy-start | bytes 3932164
  44.9 1.0 copy-start.2
  44.9 1.1 %copy-start.4 = (bf16[4,5,128,64]{2,3,1,0:T(8,128)(2,1)S(1)}, bf16[4,5,128,64]{2,3,1,0:T(8,128)(2,1)}, u32[]{:S(2)}) copy-start(bf16[4,5,128,64]{2,3,1,0:T(8,128)(2,1)} %copy-done.3) | copy-start | bytes 983044
  44.9 1.3 %copy-start.8 = (bf16[4,128,5,128]{1,3,2,0:T(8,128)(2,1)S(1)}, bf16[4,128,5,128]{1,3,2,0:T(8,128)(2,1)}, u32[]{:S(2)}) copy-start(bf16[4,128,5,128]{1,3,2,0:T(8,128)(2,1)} %get-tuple-element.83) | copy-start | bytes 1966084
  44.9 1.3 %copy-start.11 = (pred[128]{0:T(512)(128)(4,1)S(1)}, pred[128]{0:T(512)(128)(4,1)}, u32[]{:S(2)}) copy-start(pred[128]{0:T(512)(128)(4,1)} %copy-done.10) | copy-start | bytes 388
  47.4 1.7 %copy-start.5 = (f32[4,128,128]{1,2,0:T(8,128)S(1)}, f32[4,128,128]{1,2,0:T(8,128)}, u32[]{:S(2)}) copy-start(f32[4,128,128]{1,2,0:T(8,128)} %get-tuple-element.85) | copy-start | bytes 786436
Sparse Core Ops, SparseCore 0:
  44.5 21.3 reduce-scatter.1
where the time goes:
time: 99.2 us; the launch traced here: 98.3 us
  blocking collectives  47.6 us (48%)
  local copies, waits for them, and re-layouts  17.9 us (18%)
  between operations  15 us (15%)
  matrix products  13 us (13%)
  other arithmetic  4.4 us (4%)
    psum x1, blocking collectives, local(): lax.psum((jnp.sum(qgrad, 0), jnp.sum(own_grad, 0) + pre_total), ('grp', '...  41.1 us
    all_gather x1, blocking collectives, local(): prefix = lax.all_gather(prefix_own, 'grp', axis=0, tiled=True)  6.51 us
    unnamed x31, local copies, waits for them, and re-layouts  5.78 us
    dynamic_slice x16, local copies, waits for them, and re-layouts, local(): lax.map(per_group, (queries, grads, pre_keys, pre_vals, own_keys, own_vals))  4.02 us
    dot_general x4, matrix products, attend_group(): jnp.einsum('hts,sd->thd', dsb, keys, preferred_element_type=jnp.float32)  3.86 us
    dot_general x4, matrix products, attend_group(): jnp.einsum('hts,sd->thd', wts, vals, preferred_element_type=jnp.float32)  3.6 us
    dynamic_update_slice x16, local copies, waits for them, and re-layouts, local(): lax.map(per_group, (queries, grads, pre_keys, pre_vals, own_keys, own_vals))  3.37 us
    squeeze x8, local copies, waits for them, and re-layouts, local(): lax.map(per_group, (queries, grads, pre_keys, pre_vals, own_keys, own_vals))  2.9 us
  transfers between devices with their start and end apart: 1, of which 0 were waited for; matrix products, arithmetic and copies ran while one was open for 5% of the time, Pallas kernels for 0%

commit v1 on v0

v1 whole, which is shorter than its diff:
```python
import functools

import jax
import jax.numpy as jnp
from jax import lax
from jax.experimental import pallas as pl
from jax.experimental.pallas import tpu as pltpu
from jax.sharding import PartitionSpec as P

QH = 20
KVH = 4
HD = 128
NEG_BIG = -1e30
GROUP = QH // KVH
WIDTH = KVH * HD
GCOLS = GROUP * HD
MESH = pl.DeviceIdType.MESH
F32 = jnp.float32
BF16 = jnp.bfloat16

NT = (((1,), (1,)), ((), ()))
NN = (((1,), (0,)), ((), ()))
TN = (((0,), (0,)), ((), ()))


def dot(a, b, dims):
    return lax.dot_general(a, b, dims, preferred_element_type=F32)


def heads_down(x):
    return jnp.concatenate([x[:, h * HD:(h + 1) * HD] for h in range(GROUP)], axis=0)


def kernel(
    n_grp, n_dp, rows_per,
    len_ref, q_hbm, kv_hbm, pre_ref, qb_ref, kvb_ref, g_hbm,
    att_hbm, dq_hbm, dkv_hbm, dpre_ref, qsum_ref, kvsum_ref,
    q_s, g_s, kv_s, q2, g2, kv2, sown, dpown, pb_s, att_s, dq_s, dkv_s,
    pre_all, pg, pr, bs, br, b2, fin,
    in_sem, out_sem,
    ag_send, ag_recv, pg_send, pg_recv, ba_send, ba_recv, bb_send, bb_recv, bc_send, bc_recv,
):
    me = lax.axis_index("grp")
    my = lax.axis_index("dp")
    factor = HD ** (-0.5)
    slots = q_s.shape[0]
    own_rows = pre_ref.shape[0]
    pre_rows = n_grp * own_rows

    barrier = pltpu.get_barrier_semaphore()
    for off in range(1, n_grp):
        pl.semaphore_signal(barrier, inc=1, device_id={"grp": lax.rem(me + off, n_grp)}, device_id_type=MESH)
    for off in range(1, n_dp):
        pl.semaphore_signal(barrier, inc=1, device_id={"dp": lax.rem(my + off, n_dp)}, device_id_type=MESH)

    loads = [pltpu.make_async_copy(kv_hbm, kv_s, in_sem.at[0])]
    for j in range(KVH):
        cols = pl.ds(j * GCOLS, GCOLS)
        loads.append(pltpu.make_async_copy(q_hbm.at[:, cols], q_s.at[:, cols], in_sem.at[1 + 2 * j]))
        loads.append(pltpu.make_async_copy(g_hbm.at[:, cols], g_s.at[:, cols], in_sem.at[2 + 2 * j]))
    for item in loads:
        item.start()

    kvb = kvb_ref[...].reshape(1, 2 * WIDTH)
    pre_all[me] = (pre_ref[...].astype(F32) + kvb).astype(BF16)

    def exchange(axis, here, count, src, dst, send, recv):
        out = []
        for off in range(1, count):
            peer = lax.rem(here + off, count)
            out.append(pltpu.make_async_remote_copy(
                src_ref=src(peer), dst_ref=dst.at[here],
                send_sem=send.at[off - 1], recv_sem=recv.at[here],
                device_id={axis: peer}, device_id_type=MESH))
        return out

    def arrived(axis, here, count, src, dst, send, recv):
        for off in range(1, count):
            peer = lax.rem(here + off, count)
            pltpu.make_async_remote_copy(
                src_ref=src(peer), dst_ref=dst.at[peer],
                send_sem=send.at[off - 1], recv_sem=recv.at[peer],
                device_id={axis: peer}, device_id_type=MESH).wait_recv()

    ag = ("grp", me, n_grp, lambda peer: pre_all.at[me], pre_all, ag_send, ag_recv)
    ba = ("grp", me, n_grp, lambda peer: bs.at[peer], br, ba_send, ba_recv)
    rs = ("grp", me, n_grp, lambda peer: pg.at[peer], pr, pg_send, pg_recv)
    bb = ("dp", my, n_dp, lambda peer: b2.at[my], b2, bb_send, bb_recv)
    bc = ("grp", me, n_grp, lambda peer: fin.at[me], fin, bc_send, bc_recv)

    length = len_ref[0, 0]
    live_in = lax.broadcasted_iota(jnp.int32, (slots, GCOLS), 0) < length
    live_out = lax.broadcasted_iota(jnp.int32, (slots, HD), 0) < length
    key_at = lax.broadcasted_iota(jnp.int32, (slots, slots), 0)
    row_at = lax.broadcasted_iota(jnp.int32, (slots, slots), 1)
    allow = jnp.concatenate([key_at <= row_at] * GROUP, axis=1)

    pl.semaphore_wait(barrier, n_grp - 1 + n_dp - 1)
    ag_out = exchange(*ag)
    for item in ag_out:
        item.start()

    loads[0].wait()
    kv2[...] = (kv_s[...].astype(F32) + kvb).astype(BF16)
    qb = qb_ref[...].reshape(1, QH * HD)
    for j in range(KVH):
        cols = slice(j * GCOLS, (j + 1) * GCOLS)
        loads[1 + 2 * j].wait()
        loads[2 + 2 * j].wait()
        qj = heads_down((q_s[:, cols].astype(F32) + qb[:, cols]).astype(BF16))
        gj = g_s[:, cols]
        gj = heads_down(jnp.where(live_in, gj, jnp.zeros_like(gj)))
        q2[j] = qj
        g2[j] = gj
        raw = dot(kv2[:, j * HD:(j + 1) * HD], qj, NT) * factor
        sown[j] = jnp.where(allow, raw, NEG_BIG)
        dpown[j] = dot(kv2[:, WIDTH + j * HD:WIDTH + (j + 1) * HD], gj, NT)

    arrived(*ag)

    stores = []
    for j in range(KVH):
        cols = pl.ds(j * GCOLS, GCOLS)
        kc = slice(j * HD, (j + 1) * HD)
        vc = slice(WIDTH + j * HD, WIDTH + (j + 1) * HD)
        pk = pre_all[:, :, kc].reshape(pre_rows, HD)
        pv = pre_all[:, :, vc].reshape(pre_rows, HD)
        qj = q2[j]
        gj = g2[j]
        s_p = dot(pk, qj, NT) * factor
        s_o = sown[j]
        dp_p = dot(pv, gj, NT)
        dp_o = dpown[j]
        top = jnp.maximum(jnp.max(s_p, 0, keepdims=True), jnp.max(s_o, 0, keepdims=True))
        e_p = jnp.exp(s_p - top)
        e_o = jnp.exp(s_o - top)
        inv = 1.0 / (jnp.sum(e_p, 0, keepdims=True) + jnp.sum(e_o, 0, keepdims=True))
        p_p = e_p * inv
        p_o = e_o * inv
        row = jnp.sum(p_p * dp_p, 0, keepdims=True) + jnp.sum(p_o * dp_o, 0, keepdims=True)
        ds = jnp.concatenate([(p_p * (dp_p - row)).astype(BF16), (p_o * (dp_o - row)).astype(BF16)], axis=0)
        pb = jnp.concatenate([p_p.astype(BF16), p_o.astype(BF16)], axis=0)
        pb_s[j] = pb
        keys = jnp.concatenate([pk, kv2[:, kc]], axis=0)
        dk = dot(ds, qj, NN) * factor
        dv = dot(pb, gj, NN)
        dq = dot(ds, keys, TN) * factor
        for col, grad, base in ((kc, dk, QH), (vc, dv, QH + KVH)):
            rounded = grad.astype(BF16)
            pg[:, :, col] = rounded[:pre_rows].reshape(n_grp, own_rows, HD)
            dkv_s[:, col] = rounded[pre_rows:]
            at = base + j
            bs[at // rows_per, at % rows_per:at % rows_per + 1, :] = jnp.sum(grad, 0, keepdims=True)
        for h in range(GROUP):
            part = dq[h * slots:(h + 1) * slots]
            at = j * GROUP + h
            bs[at // rows_per, at % rows_per:at % rows_per + 1, :] = jnp.sum(part, 0, keepdims=True)
            dq_s[:, at * HD:(at + 1) * HD] = part.astype(BF16)
        stores.append(pltpu.make_async_copy(dq_s.at[:, cols], dq_hbm.at[:, cols], out_sem.at[1 + 2 * j]))
        stores[-1].start()

    ba_out = exchange(*ba)
    for item in ba_out:
        item.start()
    rs_out = exchange(*rs)
    for item in rs_out:
        item.start()
    stores.append(pltpu.make_async_copy(dkv_s, dkv_hbm, out_sem.at[0]))
    stores[-1].start()

    def forward(j):
        cols = pl.ds(j * GCOLS, GCOLS)
        pv = pre_all[:, :, WIDTH + j * HD:WIDTH + (j + 1) * HD].reshape(pre_rows, HD)
        vals = jnp.concatenate([pv, kv2[:, WIDTH + j * HD:WIDTH + (j + 1) * HD]], axis=0)
        out = dot(pb_s[j], vals, TN)
        for h in range(GROUP):
            at = j * GROUP + h
            att_s[:, at * HD:(at + 1) * HD] = jnp.where(live_out, out[h * slots:(h + 1) * slots], 0.0).astype(BF16)
        stores.append(pltpu.make_async_copy(att_s.at[:, cols], att_hbm.at[:, cols], out_sem.at[2 + 2 * j]))
        stores[-1].start()

    for j in range(KVH // 2):
        forward(j)

    arrived(*ba)
    br[me] = bs[me]
    total = br[0]
    for k in range(1, n_grp):
        total = total + br[k]
    b2[my] = total
    bb_out = exchange(*bb)
    for item in bb_out:
        item.start()

    for j in range(KVH // 2, KVH):
        forward(j)

    arrived(*rs)
    pr[me] = pg[me]
    acc = pr[0].astype(F32)
    for k in range(1, n_grp):
        acc = acc + pr[k].astype(F32)
    dpre_ref[...] = acc.astype(BF16)

    arrived(*bb)
    total = b2[0]
    for k in range(1, n_dp):
        total = total + b2[k]
    fin[me] = total
    bc_out = exchange(*bc)
    for item in bc_out:
        item.start()
    for item in stores:
        item.wait()
    for item in ag_out + ba_out + rs_out + bb_out:
        item.wait_send()
    arrived(*bc)
    for r in range(QH):
        qsum_ref[pl.ds(r * HD, HD)] = fin[r // rows_per, r % rows_per]
    for r in range(2 * KVH):
        at = QH + r
        kvsum_ref[pl.ds(r * HD, HD)] = fin[at // rows_per, at % rows_per]
    for item in bc_out:
        item.wait_send()


def local(n_grp, n_dp, query, resp_kv, prefix_kv, query_bias, kv_bias, out_grad, lengths):
    slots = query.shape[1]
    own_rows = prefix_kv.shape[1]
    pre_rows = own_rows * n_grp
    rows_per = -(-(QH + 2 * KVH) // n_grp)
    if n_grp * 8 >= QH + 2 * KVH:
        rows_per = min(8, 1 << (rows_per - 1).bit_length())
    tile = -(-rows_per // 8) * 8
    qw = QH * HD
    kw = 2 * WIDTH
    any_spec = pl.BlockSpec(memory_space=pl.ANY)
    vmem = pl.BlockSpec(memory_space=pltpu.VMEM)
    smem = pl.BlockSpec(memory_space=pltpu.SMEM)
    dma = lambda n: pltpu.SemaphoreType.DMA((n,))
    outs = pl.pallas_call(
        functools.partial(kernel, n_grp, n_dp, rows_per),
        name="replay",
        out_shape=(
            jax.ShapeDtypeStruct((slots, qw), BF16),
            jax.ShapeDtypeStruct((slots, qw), BF16),
            jax.ShapeDtypeStruct((slots, kw), BF16),
            jax.ShapeDtypeStruct((own_rows, kw), BF16),
            jax.ShapeDtypeStruct((qw,), F32),
            jax.ShapeDtypeStruct((kw,), F32),
        ),
        in_specs=[smem, any_spec, any_spec, vmem, vmem, vmem, any_spec],
        out_specs=(any_spec, any_spec, any_spec, vmem, vmem, vmem),
        scratch_shapes=[
            pltpu.VMEM((slots, qw), BF16),
            pltpu.VMEM((slots, qw), BF16),
            pltpu.VMEM((slots, kw), BF16),
            pltpu.VMEM((KVH, GROUP * slots, HD), BF16),
            pltpu.VMEM((KVH, GROUP * slots, HD), BF16),
            pltpu.VMEM((slots, kw), BF16),
            pltpu.VMEM((KVH, slots, GROUP * slots), F32),
            pltpu.VMEM((KVH, slots, GROUP * slots), F32),
            pltpu.VMEM((KVH, pre_rows + slots, GROUP * slots), BF16),
            pltpu.VMEM((slots, qw), BF16),
            pltpu.VMEM((slots, qw), BF16),
            pltpu.VMEM((slots, kw), BF16),
            pltpu.VMEM((n_grp, own_rows, kw), BF16),
            pltpu.VMEM((n_grp, own_rows, kw), BF16),
            pltpu.VMEM((n_grp, own_rows, kw), BF16),
            pltpu.VMEM((n_grp, tile, HD), F32),
            pltpu.VMEM((n_grp, tile, HD), F32),
            pltpu.VMEM((n_dp, tile, HD), F32),
            pltpu.VMEM((n_grp, tile, HD), F32),
            dma(1 + 2 * KVH), dma(1 + 2 * KVH),
            dma(n_grp - 1), dma(n_grp), dma(n_grp - 1), dma(n_grp),
            dma(n_grp - 1), dma(n_grp), dma(n_dp - 1), dma(n_dp),
            dma(n_grp - 1), dma(n_grp),
        ],
        compiler_params=pltpu.CompilerParams(
            collective_id=0, has_side_effects=True, vmem_limit_bytes=24 * 1024 * 1024
        ),
    )(lengths, query[0], resp_kv[0], prefix_kv[0], query_bias, kv_bias, out_grad[0])
    att, dq, dkv, dpre, qsum, kvsum = outs
    return att[None], dq[None], dkv[None], dpre[None], qsum, kvsum


def solution(mesh):
    return jax.shard_map(
        functools.partial(local, mesh.shape["grp"], mesh.shape["dp"]),
        mesh=mesh,
        in_specs=(
            P("dp", "grp", None),
            P("dp", "grp", None),
            P("dp", "grp", None),
            P(),
            P(),
            P("dp", "grp", None),
            P("dp", "grp"),
        ),
        out_specs=(
            P("dp", "grp", None),
            P("dp", "grp", None),
            P("dp", "grp", None),
            P("dp", "grp", None),
            P(),
            P(),
        ),
        check_vma=False,
    )
```

time: 99.2 us -> 31.8 us (0.32)
  blocking collectives: 47.6 us -> 0 us
  Pallas kernels: 0 us -> 20.7 us
  between operations: 15 us -> 1.3 us
  matrix products: 13 us -> 0 us
  local copies, waits for them, and re-layouts: 17.9 us -> 9.45 us
  other arithmetic: 4.4 us -> 0 us
    psum x1 -> x0, blocking collectives: 41.1 us -> none  [local(): lax.psum((jnp.sum(qgrad, 0), jnp.sum(own_grad, 0) + pre_total), ('grp', '...]
    pallas_call x0 -> x1, Pallas kernels: none -> 20.7 us  [local(): pl.pallas_call(functools.partial(kernel, n_grp, n_dp, rows_per), name='re...]
    dot_general x24 -> x0, matrix products: 11.7 us -> none  [the longest x4 3.86 us: attend_group(): jnp.einsum('hts,sd->thd', dsb, keys, preferred_element_type=jnp.float32)]
    all_gather x1 -> x0, blocking collectives: 6.51 us -> none  [local(): prefix = lax.all_gather(prefix_own, 'grp', axis=0, tiled=True)]
    dynamic_slice x16 -> x0, local copies, waits for them, and re-layouts: 4.02 us -> none  [local(): lax.map(per_group, (queries, grads, pre_keys, pre_vals, own_keys, own_vals))]
    unnamed x31 -> x18, local copies, waits for them, and re-layouts: 5.78 us -> 9.45 us
    dynamic_update_slice x16 -> x0, local copies, waits for them, and re-layouts: 3.37 us -> none  [local(): lax.map(per_group, (queries, grads, pre_keys, pre_vals, own_keys, own_vals))]
    squeeze x8 -> x0, local copies, waits for them, and re-layouts: 2.9 us -> none  [local(): lax.map(per_group, (queries, grads, pre_keys, pre_vals, own_keys, own_vals))]
  transfers between devices with their start and end apart: 1 -> 0, of which waited for: 0 -> 0; matrix products, arithmetic and copies ran while one was open for 5% -> 0% of each run, Pallas kernels for 0% -> 0%
where the time goes in v1:
time: 31.8 us; the launch traced here: 31.4 us
  Pallas kernels  20.7 us (65%)
  local copies, waits for them, and re-layouts  9.45 us (30%)
  between operations  1.3 us (4%)
    pallas_call x1, Pallas kernels, local(): pl.pallas_call(functools.partial(kernel, n_grp, n_dp, rows_per), name='re...  20.7 us
    unnamed x18, local copies, waits for them, and re-layouts  9.45 us

profile of v1, /device:TPU:0, one launch (start us, length us, event | category | flops | bytes accessed | tf_op | source)
XLA Modules:
  0.0 31.4 jit_solution(2663935869887063388)
XLA Ops:
  1.3 0.0 copy-start.5
  1.3 0.7 %copy-done.5 = f32[1024]{0:T(1024)S(1)} copy-done((f32[1024]{0:T(1024)S(1)}, f32[1024]{0:T(1024)}, u32[]{:S(2)}) %copy-start.5) | copy-done | bytes 4120
  2.0 0.0 copy-start
  2.0 1.1 %copy-done = bf16[1,128,2560]{2,1,0:T(8,128)(2,1)S(1)} copy-done((bf16[1,128,2560]{2,1,0:T(8,128)(2,1)S(1)}, bf16[1,128,2560]{2,1,0:T(8,128)(2,1)}, u32[]{:S(2)}) %copy-start) | copy-done | bytes 655384
  3.1 0.0 copy-start.1
  3.1 1.1 %copy-done.1 = bf16[1,128,2560]{2,1,0:T(8,128)(2,1)S(1)} copy-done((bf16[1,128,2560]{2,1,0:T(8,128)(2,1)S(1)}, bf16[1,128,2560]{2,1,0:T(8,128)(2,1)}, u32[]{:S(2)}) %copy-start.1) | copy-done | bytes 655384
  4.1 0.0 copy-start.2
  4.1 0.9 %copy-done.2 = bf16[1,128,1024]{2,1,0:T(8,128)(2,1)S(1)} copy-done((bf16[1,128,1024]{2,1,0:T(8,128)(2,1)S(1)}, bf16[1,128,1024]{2,1,0:T(8,128)(2,1)}, u32[]{:S(2)}) %copy-start.2) | copy-done | bytes 262168
  5.1 0.0 copy-start.3
  5.1 0.8 %copy-done.3 = bf16[1,16,1024]{2,1,0:T(8,128)(2,1)S(1)} copy-done((bf16[1,16,1024]{2,1,0:T(8,128)(2,1)S(1)}, bf16[1,16,1024]{2,1,0:T(8,128)(2,1)}, u32[]{:S(2)}) %copy-start.3) | copy-done | bytes 32792
  5.9 0.0 copy-start.4
  5.9 0.7 %copy-done.4 = f32[2560]{0:T(1024)S(1)} copy-done((f32[2560]{0:T(1024)S(1)}, f32[2560]{0:T(1024)}, u32[]{:S(2)}) %copy-start.4) | copy-done | bytes 10264
  6.6 20.7 %replay.1 = (bf16[128,2560]{1,0:T(8,128)(2,1)S(1)}, bf16[128,2560]{1,0:T(8,128)(2,1)S(1)}, bf16[128,1024]{1,0:T(8,128)(2,1)S(1)}, bf16[16,1024]{1,0:T(8,128)(2,1...) custom-call(s32[1,1]{1,0:T(1,128)S(6)} %copy.19.len_ref, bf16[128,2560]{1,0:T(8,128)(2,1)S(1)} %bitcast.8, ...), custom_call_target="tpu_custom_call" | custom-call | tf_op jit(solution)/shard_map/replay/pallas_call | solution.py:241
  27.3 0.8 %copy.20 = bf16[1,128,2560]{2,1,0:T(8,128)(2,1)} copy(bf16[1,128,2560]{2,1,0:T(8,128)(2,1)S(1)} %bitcast.11) | data formatting | bytes 1310720
  28.1 0.8 %copy.21 = bf16[1,128,2560]{2,1,0:T(8,128)(2,1)} copy(bf16[1,128,2560]{2,1,0:T(8,128)(2,1)S(1)} %bitcast.10) | data formatting | bytes 1310720
  28.9 0.7 %copy.22 = bf16[1,128,1024]{2,1,0:T(8,128)(2,1)} copy(bf16[1,128,1024]{2,1,0:T(8,128)(2,1)S(1)} %bitcast.12) | data formatting | bytes 524288
  29.6 0.6 %copy.23 = bf16[1,16,1024]{2,1,0:T(8,128)(2,1)} copy(bf16[1,16,1024]{2,1,0:T(8,128)(2,1)S(1)} %bitcast.15) | data formatting | bytes 65536
  30.3 0.6 %copy.24 = f32[2560]{0:T(1024)} copy(f32[2560]{0:T(1024)S(1)} %get-tuple-element.28) | data formatting | bytes 20480
  30.9 0.6 %copy.25 = f32[1024]{0:T(1024)} copy(f32[1024]{0:T(1024)S(1)} %get-tuple-element.29) | data formatting | bytes 8192
Async XLA Ops:
  1.3 0.7 %copy-start.5 = (f32[1024]{0:T(1024)S(1)}, f32[1024]{0:T(1024)}, u32[]{:S(2)}) copy-start(f32[1024]{0:T(1024)} %kvb_ref.1) | copy-start | bytes 12292
  2.0 1.1 %copy-start = (bf16[1,128,2560]{2,1,0:T(8,128)(2,1)S(1)}, bf16[1,128,2560]{2,1,0:T(8,128)(2,1)}, u32[]{:S(2)}) copy-start(bf16[1,128,2560]{2,1,0:T(8,128)(2,1)} %param.7) | copy-start | bytes 1966084
  3.1 1.1 %copy-start.1 = (bf16[1,128,2560]{2,1,0:T(8,128)(2,1)S(1)}, bf16[1,128,2560]{2,1,0:T(8,128)(2,1)}, u32[]{:S(2)}) copy-start(bf16[1,128,2560]{2,1,0:T(8,128)(2,1)} %param.12) | copy-start | bytes 1966084
  4.1 0.9 %copy-start.2 = (bf16[1,128,1024]{2,1,0:T(8,128)(2,1)S(1)}, bf16[1,128,1024]{2,1,0:T(8,128)(2,1)}, u32[]{:S(2)}) copy-start(bf16[1,128,1024]{2,1,0:T(8,128)(2,1)} %param.8) | copy-start | bytes 786436
  5.1 0.8 %copy-start.3 = (bf16[1,16,1024]{2,1,0:T(8,128)(2,1)S(1)}, bf16[1,16,1024]{2,1,0:T(8,128)(2,1)}, u32[]{:S(2)}) copy-start(bf16[1,16,1024]{2,1,0:T(8,128)(2,1)} %param.9) | copy-start | bytes 98308
  5.9 0.7 %copy-start.4 = (f32[2560]{0:T(1024)S(1)}, f32[2560]{0:T(1024)}, u32[]{:S(2)}) copy-start(f32[2560]{0:T(1024)} %qb_ref.1) | copy-start | bytes 30724

commit v2 on v1

v2 whole, which is shorter than its diff:
```python
import functools

import jax
import jax.numpy as jnp
from jax import lax
from jax.experimental import pallas as pl
from jax.experimental.pallas import tpu as pltpu
from jax.sharding import PartitionSpec as P

QH = 20
KVH = 4
HD = 128
NEG_BIG = -1e30
GROUP = QH // KVH
WIDTH = KVH * HD
GCOLS = GROUP * HD
MESH = pl.DeviceIdType.MESH
F32 = jnp.float32
BF16 = jnp.bfloat16

NT = (((1,), (1,)), ((), ()))
NN = (((1,), (0,)), ((), ()))
TN = (((0,), (0,)), ((), ()))


def dot(a, b, dims):
    return lax.dot_general(a, b, dims, preferred_element_type=F32)


def heads_down(x):
    return jnp.concatenate([x[:, h * HD:(h + 1) * HD] for h in range(GROUP)], axis=0)


def kernel(
    n_grp, n_dp, rows_per,
    len_ref, q_hbm, kv_hbm, pre_hbm, qb_hbm, kvb_hbm, g_hbm,
    att_s, dq_s, dkv_s, dpre_ref, qsum_ref, kvsum_ref,
    pre_ref, qb_ref, kvb_ref, q_s, g_s, kv_s, q2, g2, kv2, sown, dpown, pb_s,
    pre_all, pg, pr, bs, br, b2, fin,
    in_sem,
    ag_send, ag_recv, pg_send, pg_recv, ba_send, ba_recv, bb_send, bb_recv, bc_send, bc_recv,
):
    me = lax.axis_index("grp")
    my = lax.axis_index("dp")
    factor = HD ** (-0.5)
    slots = q_s.shape[0]
    own_rows = pre_ref.shape[0]
    pre_rows = n_grp * own_rows

    barrier = pltpu.get_barrier_semaphore()
    for off in range(1, n_grp):
        pl.semaphore_signal(barrier, inc=1, device_id={"grp": lax.rem(me + off, n_grp)}, device_id_type=MESH)
    for off in range(1, n_dp):
        pl.semaphore_signal(barrier, inc=1, device_id={"dp": lax.rem(my + off, n_dp)}, device_id_type=MESH)

    base = 1 + 2 * KVH
    small = [
        pltpu.make_async_copy(src, dst, in_sem.at[base + k])
        for k, (src, dst) in enumerate(
            ((pre_hbm, pre_ref), (kvb_hbm, kvb_ref), (qb_hbm, qb_ref)))
    ]
    loads = [pltpu.make_async_copy(kv_hbm, kv_s, in_sem.at[0])]
    for j in range(KVH):
        cols = pl.ds(j * GCOLS, GCOLS)
        loads.append(pltpu.make_async_copy(q_hbm.at[:, cols], q_s.at[:, cols], in_sem.at[1 + 2 * j]))
        loads.append(pltpu.make_async_copy(g_hbm.at[:, cols], g_s.at[:, cols], in_sem.at[2 + 2 * j]))
    for item in small + loads:
        item.start()
    small[0].wait()
    small[1].wait()
    kvb = kvb_ref[...].reshape(1, 2 * WIDTH)
    mine = (pre_ref[...].astype(F32) + kvb).astype(BF16)
    for j in range(KVH):
        pre_all[j, me] = jnp.concatenate(
            [mine[:, j * HD:(j + 1) * HD], mine[:, WIDTH + j * HD:WIDTH + (j + 1) * HD]], axis=1)
    small[2].wait()

    sent = []

    def exchange(axis, here, count, src, dst, send, recv):
        for off in range(1, count):
            peer = lax.rem(here + off, count)
            sent.append(pltpu.make_async_remote_copy(
                src_ref=src(peer), dst_ref=dst.at[here],
                send_sem=send.at[off - 1], recv_sem=recv.at[here],
                device_id={axis: peer}, device_id_type=MESH))
            sent[-1].start()

    def arrived(axis, here, count, src, dst, send, recv):
        for off in range(1, count):
            peer = lax.rem(here + off, count)
            pltpu.make_async_remote_copy(
                src_ref=src(peer), dst_ref=dst.at[peer],
                send_sem=send.at[off - 1], recv_sem=recv.at[peer],
                device_id={axis: peer}, device_id_type=MESH).wait_recv()

    ag = [("grp", me, n_grp, lambda peer, j=j: pre_all.at[j, me], pre_all.at[j], ag_send.at[j], ag_recv.at[j])
          for j in range(KVH)]
    rs = [("grp", me, n_grp, lambda peer, j=j: pg.at[j, peer], pr.at[j], pg_send.at[j], pg_recv.at[j])
          for j in range(KVH)]
    ba = ("grp", me, n_grp, lambda peer: bs.at[peer], br, ba_send, ba_recv)
    bb = ("dp", my, n_dp, lambda peer: b2.at[my], b2, bb_send, bb_recv)
    bc = ("grp", me, n_grp, lambda peer: fin.at[me], fin, bc_send, bc_recv)

    length = len_ref[0, 0]
    live_in = lax.broadcasted_iota(jnp.int32, (slots, GCOLS), 0) < length
    live_out = lax.broadcasted_iota(jnp.int32, (slots, HD), 0) < length
    key_at = lax.broadcasted_iota(jnp.int32, (slots, slots), 0)
    row_at = lax.broadcasted_iota(jnp.int32, (slots, slots), 1)
    allow = jnp.concatenate([key_at <= row_at] * GROUP, axis=1)

    loads[0].wait()
    kv2[...] = (kv_s[...].astype(F32) + kvb).astype(BF16)
    qb = qb_ref[...].reshape(1, QH * HD)
    def ready(j):
        cols = slice(j * GCOLS, (j + 1) * GCOLS)
        loads[1 + 2 * j].wait()
        loads[2 + 2 * j].wait()
        qj = heads_down((q_s[:, cols].astype(F32) + qb[:, cols]).astype(BF16))
        gj = g_s[:, cols]
        gj = heads_down(jnp.where(live_in, gj, jnp.zeros_like(gj)))
        q2[j] = qj
        g2[j] = gj
        raw = dot(kv2[:, j * HD:(j + 1) * HD], qj, NT) * factor
        sown[j] = jnp.where(allow, raw, NEG_BIG)
        dpown[j] = dot(kv2[:, WIDTH + j * HD:WIDTH + (j + 1) * HD], gj, NT)

    ready(0)
    pl.semaphore_wait(barrier, n_grp - 1 + n_dp - 1)
    for j in range(KVH):
        exchange(*ag[j])
    for j in range(1, KVH):
        ready(j)

    for j in range(KVH):
        arrived(*ag[j])
        kc = slice(j * HD, (j + 1) * HD)
        vc = slice(WIDTH + j * HD, WIDTH + (j + 1) * HD)
        both = pre_all[j].reshape(pre_rows, 2 * HD)
        pk = both[:, :HD]
        pv = both[:, HD:]
        qj = q2[j]
        gj = g2[j]
        s_p = dot(pk, qj, NT) * factor
        s_o = sown[j]
        dp_p = dot(pv, gj, NT)
        dp_o = dpown[j]
        top = jnp.maximum(jnp.max(s_p, 0, keepdims=True), jnp.max(s_o, 0, keepdims=True))
        e_p = jnp.exp(s_p - top)
        e_o = jnp.exp(s_o - top)
        inv = 1.0 / (jnp.sum(e_p, 0, keepdims=True) + jnp.sum(e_o, 0, keepdims=True))
        p_p = e_p * inv
        p_o = e_o * inv
        row = jnp.sum(p_p * dp_p, 0, keepdims=True) + jnp.sum(p_o * dp_o, 0, keepdims=True)
        ds = jnp.concatenate([(p_p * (dp_p - row)).astype(BF16), (p_o * (dp_o - row)).astype(BF16)], axis=0)
        pb = jnp.concatenate([p_p.astype(BF16), p_o.astype(BF16)], axis=0)
        pb_s[j] = pb
        keys = jnp.concatenate([pk, kv2[:, kc]], axis=0)
        dk = dot(ds, qj, NN) * factor
        dv = dot(pb, gj, NN)
        dq = dot(ds, keys, TN) * factor
        dkr = dk.astype(BF16)
        dvr = dv.astype(BF16)
        pg[j] = jnp.concatenate([dkr[:pre_rows], dvr[:pre_rows]], axis=1).reshape(n_grp, own_rows, 2 * HD)
        exchange(*rs[j])
        dkv_s[:, kc] = dkr[pre_rows:]
        dkv_s[:, vc] = dvr[pre_rows:]
        for at, grad in ((QH + j, dk), (QH + KVH + j, dv)):
            bs[at // rows_per, at % rows_per:at % rows_per + 1, :] = jnp.sum(grad, 0, keepdims=True)
        for h in range(GROUP):
            part = dq[h * slots:(h + 1) * slots]
            at = j * GROUP + h
            bs[at // rows_per, at % rows_per:at % rows_per + 1, :] = jnp.sum(part, 0, keepdims=True)
            dq_s[:, at * HD:(at + 1) * HD] = part.astype(BF16)

    exchange(*ba)

    def forward(j):
        pv = pre_all[j].reshape(pre_rows, 2 * HD)[:, HD:]
        vals = jnp.concatenate([pv, kv2[:, WIDTH + j * HD:WIDTH + (j + 1) * HD]], axis=0)
        out = dot(pb_s[j], vals, TN)
        for h in range(GROUP):
            at = j * GROUP + h
            att_s[:, at * HD:(at + 1) * HD] = jnp.where(live_out, out[h * slots:(h + 1) * slots], 0.0).astype(BF16)

    for j in range(KVH // 2):
        forward(j)

    arrived(*ba)
    br[me] = bs[me]
    total = br[0]
    for k in range(1, n_grp):
        total = total + br[k]
    b2[my] = total
    exchange(*bb)

    for j in range(KVH // 2, KVH):
        forward(j)

    for j in range(KVH):
        arrived(*rs[j])
        pr[j, me] = pg[j, me]
        acc = pr[j, 0].astype(F32)
        for k in range(1, n_grp):
            acc = acc + pr[j, k].astype(F32)
        acc = acc.astype(BF16)
        dpre_ref[:, j * HD:(j + 1) * HD] = acc[:, :HD]
        dpre_ref[:, WIDTH + j * HD:WIDTH + (j + 1) * HD] = acc[:, HD:]

    arrived(*bb)
    total = b2[0]
    for k in range(1, n_dp):
        total = total + b2[k]
    fin[me] = total
    exchange(*bc)
    for item in sent:
        item.wait_send()
    arrived(*bc)
    for r in range(QH):
        qsum_ref[pl.ds(r * HD, HD)] = fin[r // rows_per, r % rows_per]
    for r in range(2 * KVH):
        at = QH + r
        kvsum_ref[pl.ds(r * HD, HD)] = fin[at // rows_per, at % rows_per]


def write_out(*refs):
    count = (len(refs) - 1) // 2
    copies = [pltpu.make_async_copy(refs[k], refs[count + k], refs[-1].at[k]) for k in range(count)]
    for item in copies:
        item.start()
    for item in copies:
        item.wait()


def local(n_grp, n_dp, query, resp_kv, prefix_kv, query_bias, kv_bias, out_grad, lengths):
    slots = query.shape[1]
    own_rows = prefix_kv.shape[1]
    pre_rows = own_rows * n_grp
    rows_per = -(-(QH + 2 * KVH) // n_grp)
    if n_grp * 8 >= QH + 2 * KVH:
        rows_per = min(8, 1 << (rows_per - 1).bit_length())
    tile = -(-rows_per // 8) * 8
    qw = QH * HD
    kw = 2 * WIDTH
    hbm = pl.BlockSpec(memory_space=pltpu.HBM)
    vmem = pl.BlockSpec(memory_space=pltpu.VMEM)
    dma = lambda *n: pltpu.SemaphoreType.DMA(n)
    shapes = (
        jax.ShapeDtypeStruct((slots, qw), BF16),
        jax.ShapeDtypeStruct((slots, qw), BF16),
        jax.ShapeDtypeStruct((slots, kw), BF16),
        jax.ShapeDtypeStruct((own_rows, kw), BF16),
        jax.ShapeDtypeStruct((qw,), F32),
        jax.ShapeDtypeStruct((kw,), F32),
    )
    outs = pl.pallas_call(
        functools.partial(kernel, n_grp, n_dp, rows_per),
        name="replay",
        out_shape=shapes,
        in_specs=[pl.BlockSpec(memory_space=pltpu.SMEM)] + [hbm] * 6,
        out_specs=(vmem,) * 6,
        scratch_shapes=[
            pltpu.VMEM((own_rows, kw), BF16),
            pltpu.VMEM((qw,), F32),
            pltpu.VMEM((kw,), F32),
            pltpu.VMEM((slots, qw), BF16),
            pltpu.VMEM((slots, qw), BF16),
            pltpu.VMEM((slots, kw), BF16),
            pltpu.VMEM((KVH, GROUP * slots, HD), BF16),
            pltpu.VMEM((KVH, GROUP * slots, HD), BF16),
            pltpu.VMEM((slots, kw), BF16),
            pltpu.VMEM((KVH, slots, GROUP * slots), F32),
            pltpu.VMEM((KVH, slots, GROUP * slots), F32),
            pltpu.VMEM((KVH, pre_rows + slots, GROUP * slots), BF16),
            pltpu.VMEM((KVH, n_grp, own_rows, 2 * HD), BF16),
            pltpu.VMEM((KVH, n_grp, own_rows, 2 * HD), BF16),
            pltpu.VMEM((KVH, n_grp, own_rows, 2 * HD), BF16),
            pltpu.VMEM((n_grp, tile, HD), F32),
            pltpu.VMEM((n_grp, tile, HD), F32),
            pltpu.VMEM((n_dp, tile, HD), F32),
            pltpu.VMEM((n_grp, tile, HD), F32),
            dma(4 + 2 * KVH),
            dma(KVH, n_grp - 1), dma(KVH, n_grp), dma(KVH, n_grp - 1), dma(KVH, n_grp),
            dma(n_grp - 1), dma(n_grp), dma(n_dp - 1), dma(n_dp),
            dma(n_grp - 1), dma(n_grp),
        ],
        compiler_params=pltpu.CompilerParams(
            collective_id=0, has_side_effects=True, vmem_limit_bytes=24 * 1024 * 1024
        ),
    )(lengths, *(pltpu.with_memory_space_constraint(x, pltpu.HBM) for x in (query[0], resp_kv[0], prefix_kv[0], query_bias, kv_bias, out_grad[0])))
    att, dq, dkv, dpre, qsum, kvsum = pl.pallas_call(
        write_out,
        name="write_out",
        out_shape=shapes,
        in_specs=[vmem] * 6,
        out_specs=(hbm,) * 6,
        scratch_shapes=[dma(6)],
        compiler_params=pltpu.CompilerParams(vmem_limit_bytes=1024 * 1024),
    )(*outs)
    return att[None], dq[None], dkv[None], dpre[None], qsum, kvsum


def solution(mesh):
    return jax.shard_map(
        functools.partial(local, mesh.shape["grp"], mesh.shape["dp"]),
        mesh=mesh,
        in_specs=(
            P("dp", "grp", None),
            P("dp", "grp", None),
            P("dp", "grp", None),
            P(),
            P(),
            P("dp", "grp", None),
            P("dp", "grp"),
        ),
        out_specs=(
            P("dp", "grp", None),
            P("dp", "grp", None),
            P("dp", "grp", None),
            P("dp", "grp", None),
            P(),
            P(),
        ),
        check_vma=False,
    )
```

time: 31.8 us -> 24.1 us (0.76)
  local copies, waits for them, and re-layouts: 9.45 us -> 0 us
  Pallas kernels: 20.7 us -> 22.7 us
    unnamed x18 -> x0, local copies, waits for them, and re-layouts: 9.45 us -> none
    pallas_call x0 -> x1, Pallas kernels: none -> 1.2 us  [local(): pl.pallas_call(write_out, name='write_out', out_shape=shapes, in_specs=[v...]
    pallas_call x1, Pallas kernels: 20.7 us -> 21.5 us  [local(): pl.pallas_call(functools.partial(kernel, n_grp, n_dp, rows_per), name='re...]
where the time goes in v2:
time: 24.1 us; the launch traced here: 23.9 us
  Pallas kernels  22.7 us (94%)
  between operations  1.29 us (5%)
    pallas_call x1, Pallas kernels, local(): pl.pallas_call(functools.partial(kernel, n_grp, n_dp, rows_per), name='re...  21.5 us
    pallas_call x1, Pallas kernels, local(): pl.pallas_call(write_out, name='write_out', out_shape=shapes, in_specs=[v...  1.2 us

profile of v2, /device:TPU:0, one launch (start us, length us, event | category | flops | bytes accessed | tf_op | source)
XLA Modules:
  0.0 23.9 jit_solution(5562175838745651692)
XLA Ops:
  1.3 21.5 %replay.1 = (bf16[128,2560]{1,0:T(8,128)(2,1)S(1)}, bf16[128,2560]{1,0:T(8,128)(2,1)S(1)}, bf16[128,1024]{1,0:T(8,128)(2,1)S(1)}, bf16[16,1024]{1,0:T(8,128)(2,1...) custom-call(s32[1,1]{1,0:T(1,128)S(6)} %copy.13.len_ref, bf16[128,2560]{1,0:T(8,128)(2,1)} %bitcast.8, ...), custom_call_target="tpu_custom_call" | custom-call | tf_op jit(solution)/shard_map/replay/pallas_call | solution.py:256
  22.7 1.2 %write_out.1 = (bf16[128,2560]{1,0:T(8,128)(2,1)}, bf16[128,2560]{1,0:T(8,128)(2,1)}, bf16[128,1024]{1,0:T(8,128)(2,1)}, bf16[16,1024]{1,0:T(8,128)(2,1)}, f32[2560]{0:T(1024)}, /*index=5*/f32[1024]{0:T(1024)}) custom-call(bf16[128,2560]{1,0:T(8,128)(2,1)S(1)} %get-tuple-element.18.refs_0_, bf16[128,2560]{1,0:T(8,128)(2,1)S(1)} %get-tuple-element.19.refs_1_, ...), custom_call_target="tpu_custom_call" | custom-call | tf_op jit(solution)/shard_map/write_out/pallas_call | solution.py:291

commit v3 on v2

--- a/solution.py
+++ b/solution.py
@@ -9,6 +9,7 @@
 
 QH = 20
 KVH = 4
+STEP = 2
 HD = 128
 NEG_BIG = -1e30
 GROUP = QH // KVH
@@ -133,7 +134,9 @@
         ready(j)
 
     for j in range(KVH):
-        arrived(*ag[j])
+        if j % STEP == 0:
+            for k in range(j, j + STEP):
+                arrived(*ag[k])
         kc = slice(j * HD, (j + 1) * HD)
         vc = slice(WIDTH + j * HD, WIDTH + (j + 1) * HD)
         both = pre_all[j].reshape(pre_rows, 2 * HD)
@@ -162,7 +165,6 @@
         dkr = dk.astype(BF16)
         dvr = dv.astype(BF16)
         pg[j] = jnp.concatenate([dkr[:pre_rows], dvr[:pre_rows]], axis=1).reshape(n_grp, own_rows, 2 * HD)
-        exchange(*rs[j])
         dkv_s[:, kc] = dkr[pre_rows:]
         dkv_s[:, vc] = dvr[pre_rows:]
         for at, grad in ((QH + j, dk), (QH + KVH + j, dv)):
@@ -172,8 +174,11 @@
             at = j * GROUP + h
             bs[at // rows_per, at % rows_per:at % rows_per + 1, :] = jnp.sum(part, 0, keepdims=True)
             dq_s[:, at * HD:(at + 1) * HD] = part.astype(BF16)
-
-    exchange(*ba)
+        if j == KVH - 1:
+            exchange(*ba)
+        if j % STEP == STEP - 1:
+            for k in range(j + 1 - STEP, j + 1):
+                exchange(*rs[k])
 
     def forward(j):
         pv = pre_all[j].reshape(pre_rows, 2 * HD)[:, HD:]

time: 24.1 us -> 23.7 us (0.983)
  Pallas kernels: 22.7 us -> 22.3 us
    pallas_call x1, Pallas kernels: 21.5 us -> 21.1 us  [local(): pl.pallas_call(functools.partial(kernel, n_grp, n_dp, rows_per), name='re...]
where the time goes in v3:
time: 23.7 us; the launch traced here: 23.6 us
  Pallas kernels  22.3 us (94%)
  between operations  1.29 us (5%)
    pallas_call x1, Pallas kernels, local(): pl.pallas_call(functools.partial(kernel, n_grp, n_dp, rows_per), name='re...  21.1 us
    pallas_call x1, Pallas kernels, local(): pl.pallas_call(write_out, name='write_out', out_shape=shapes, in_specs=[v...  1.2 us

profile of v3, /device:TPU:0, one launch (start us, length us, event | category | flops | bytes accessed | tf_op | source)
XLA Modules:
  0.0 23.6 jit_solution(4250998801412785405)
XLA Ops:
  1.3 21.1 %replay.1 = (bf16[128,2560]{1,0:T(8,128)(2,1)S(1)}, bf16[128,2560]{1,0:T(8,128)(2,1)S(1)}, bf16[128,1024]{1,0:T(8,128)(2,1)S(1)}, bf16[16,1024]{1,0:T(8,128)(2,1...) custom-call(s32[1,1]{1,0:T(1,128)S(6)} %copy.13.len_ref, bf16[128,2560]{1,0:T(8,128)(2,1)} %bitcast.8, ...), custom_call_target="tpu_custom_call" | custom-call | tf_op jit(solution)/shard_map/replay/pallas_call | solution.py:261
  22.4 1.2 %write_out.1 = (bf16[128,2560]{1,0:T(8,128)(2,1)}, bf16[128,2560]{1,0:T(8,128)(2,1)}, bf16[128,1024]{1,0:T(8,128)(2,1)}, bf16[16,1024]{1,0:T(8,128)(2,1)}, f32[2560]{0:T(1024)}, /*index=5*/f32[1024]{0:T(1024)}) custom-call(bf16[128,2560]{1,0:T(8,128)(2,1)S(1)} %get-tuple-element.18.refs_0_, bf16[128,2560]{1,0:T(8,128)(2,1)S(1)} %get-tuple-element.19.refs_1_, ...), custom_call_target="tpu_custom_call" | custom-call | tf_op jit(solution)/shard_map/write_out/pallas_call | solution.py:296

commit v4 on v3

--- a/solution.py
+++ b/solution.py
@@ -10,6 +10,7 @@
 QH = 20
 KVH = 4
 STEP = 2
+LOG2E = 1.4426950408889634
 HD = 128
 NEG_BIG = -1e30
 GROUP = QH // KVH
@@ -32,28 +33,20 @@
     return jnp.concatenate([x[:, h * HD:(h + 1) * HD] for h in range(GROUP)], axis=0)
 
 
-def kernel(
-    n_grp, n_dp, rows_per,
+def prepare(
+    n_grp,
     len_ref, q_hbm, kv_hbm, pre_hbm, qb_hbm, kvb_hbm, g_hbm,
-    att_s, dq_s, dkv_s, dpre_ref, qsum_ref, kvsum_ref,
-    pre_ref, qb_ref, kvb_ref, q_s, g_s, kv_s, q2, g2, kv2, sown, dpown, pb_s,
-    pre_all, pg, pr, bs, br, b2, fin,
-    in_sem,
-    ag_send, ag_recv, pg_send, pg_recv, ba_send, ba_recv, bb_send, bb_recv, bc_send, bc_recv,
+    q2, g2, kv2, sown, dpown, pre_all,
+    pre_ref, qb_ref, kvb_ref, q_s, g_s, kv_s, in_sem, ag_send, ag_recv,
 ):
     me = lax.axis_index("grp")
-    my = lax.axis_index("dp")
     factor = HD ** (-0.5)
+    base2 = factor * LOG2E
     slots = q_s.shape[0]
-    own_rows = pre_ref.shape[0]
-    pre_rows = n_grp * own_rows
 
     barrier = pltpu.get_barrier_semaphore()
     for off in range(1, n_grp):
         pl.semaphore_signal(barrier, inc=1, device_id={"grp": lax.rem(me + off, n_grp)}, device_id_type=MESH)
-    for off in range(1, n_dp):
-        pl.semaphore_signal(barrier, inc=1, device_id={"dp": lax.rem(my + off, n_dp)}, device_id_type=MESH)
-
     base = 1 + 2 * KVH
     small = [
         pltpu.make_async_copy(src, dst, in_sem.at[base + k])
@@ -97,15 +90,9 @@
 
     ag = [("grp", me, n_grp, lambda peer, j=j: pre_all.at[j, me], pre_all.at[j], ag_send.at[j], ag_recv.at[j])
           for j in range(KVH)]
-    rs = [("grp", me, n_grp, lambda peer, j=j: pg.at[j, peer], pr.at[j], pg_send.at[j], pg_recv.at[j])
-          for j in range(KVH)]
-    ba = ("grp", me, n_grp, lambda peer: bs.at[peer], br, ba_send, ba_recv)
-    bb = ("dp", my, n_dp, lambda peer: b2.at[my], b2, bb_send, bb_recv)
-    bc = ("grp", me, n_grp, lambda peer: fin.at[me], fin, bc_send, bc_recv)
 
     length = len_ref[0, 0]
     live_in = lax.broadcasted_iota(jnp.int32, (slots, GCOLS), 0) < length
-    live_out = lax.broadcasted_iota(jnp.int32, (slots, HD), 0) < length
     key_at = lax.broadcasted_iota(jnp.int32, (slots, slots), 0)
     row_at = lax.broadcasted_iota(jnp.int32, (slots, slots), 1)
     allow = jnp.concatenate([key_at <= row_at] * GROUP, axis=1)
@@ -122,21 +109,72 @@
         gj = heads_down(jnp.where(live_in, gj, jnp.zeros_like(gj)))
         q2[j] = qj
         g2[j] = gj
-        raw = dot(kv2[:, j * HD:(j + 1) * HD], qj, NT) * factor
+        raw = dot(kv2[:, j * HD:(j + 1) * HD], qj, NT) * base2
         sown[j] = jnp.where(allow, raw, NEG_BIG)
         dpown[j] = dot(kv2[:, WIDTH + j * HD:WIDTH + (j + 1) * HD], gj, NT)
 
     ready(0)
-    pl.semaphore_wait(barrier, n_grp - 1 + n_dp - 1)
+    pl.semaphore_wait(barrier, n_grp - 1)
     for j in range(KVH):
         exchange(*ag[j])
     for j in range(1, KVH):
         ready(j)
-
-    for j in range(KVH):
-        if j % STEP == 0:
-            for k in range(j, j + STEP):
-                arrived(*ag[k])
+    for j in range(KVH):
+        arrived(*ag[j])
+    for item in sent:
+        item.wait_send()
+
+
+def kernel(
+    n_grp, n_dp, rows_per,
+    len_ref, q2, g2, kv2, sown, dpown, pre_all,
+    att_s, dq_s, dkv_s, dpre_ref, qsum_ref, kvsum_ref,
+    pb_s, pg, pr, bs, br, b2, fin,
+    pg_send, pg_recv, ba_send, ba_recv, bb_send, bb_recv, bc_send, bc_recv,
+):
+    me = lax.axis_index("grp")
+    factor = HD ** (-0.5)
+    base2 = factor * LOG2E
+    my = lax.axis_index("dp")
+    slots = kv2.shape[0]
+    own_rows = dpre_ref.shape[0]
+    pre_rows = n_grp * own_rows
+
+    barrier = pltpu.get_barrier_semaphore()
+    for off in range(1, n_grp):
+        pl.semaphore_signal(barrier, inc=1, device_id={"grp": lax.rem(me + off, n_grp)}, device_id_type=MESH)
+    for off in range(1, n_dp):
+        pl.semaphore_signal(barrier, inc=1, device_id={"dp": lax.rem(my + off, n_dp)}, device_id_type=MESH)
+
+    sent = []
+
+    def exchange(axis, here, count, src, dst, send, recv):
+        for off in range(1, count):
+            peer = lax.rem(here + off, count)
+            sent.append(pltpu.make_async_remote_copy(
+                src_ref=src(peer), dst_ref=dst.at[here],
+                send_sem=send.at[off - 1], recv_sem=recv.at[here],
+                device_id={axis: peer}, device_id_type=MESH))
+            sent[-1].start()
+
+    def arrived(axis, here, count, src, dst, send, recv):
+        for off in range(1, count):
+            peer = lax.rem(here + off, count)
+            pltpu.make_async_remote_copy(
+                src_ref=src(peer), dst_ref=dst.at[peer],
+                send_sem=send.at[off - 1], recv_sem=recv.at[peer],
+                device_id={axis: peer}, device_id_type=MESH).wait_recv()
+
+    rs = [("grp", me, n_grp, lambda peer, j=j: pg.at[j, peer], pr.at[j], pg_send.at[j], pg_recv.at[j])
+          for j in range(KVH)]
+    ba = ("grp", me, n_grp, lambda peer: bs.at[peer], br, ba_send, ba_recv)
+    bb = ("dp", my, n_dp, lambda peer: b2.at[my], b2, bb_send, bb_recv)
+    bc = ("grp", me, n_grp, lambda peer: fin.at[me], fin, bc_send, bc_recv)
+
+    length = len_ref[0, 0]
+    live_out = lax.broadcasted_iota(jnp.int32, (slots, HD), 0) < length
+
+    for j in range(KVH):
         kc = slice(j * HD, (j + 1) * HD)
         vc = slice(WIDTH + j * HD, WIDTH + (j + 1) * HD)
         both = pre_all[j].reshape(pre_rows, 2 * HD)
@@ -144,13 +182,13 @@
         pv = both[:, HD:]
         qj = q2[j]
         gj = g2[j]
-        s_p = dot(pk, qj, NT) * factor
+        s_p = dot(pk, qj, NT) * base2
         s_o = sown[j]
         dp_p = dot(pv, gj, NT)
         dp_o = dpown[j]
         top = jnp.maximum(jnp.max(s_p, 0, keepdims=True), jnp.max(s_o, 0, keepdims=True))
-        e_p = jnp.exp(s_p - top)
-        e_o = jnp.exp(s_o - top)
+        e_p = jnp.exp2(s_p - top)
+        e_o = jnp.exp2(s_o - top)
         inv = 1.0 / (jnp.sum(e_p, 0, keepdims=True) + jnp.sum(e_o, 0, keepdims=True))
         p_p = e_p * inv
         p_o = e_o * inv
@@ -174,6 +212,8 @@
             at = j * GROUP + h
             bs[at // rows_per, at % rows_per:at % rows_per + 1, :] = jnp.sum(part, 0, keepdims=True)
             dq_s[:, at * HD:(at + 1) * HD] = part.astype(BF16)
+        if j == STEP - 1:
+            pl.semaphore_wait(barrier, n_grp - 1 + n_dp - 1)
         if j == KVH - 1:
             exchange(*ba)
         if j % STEP == STEP - 1:
@@ -258,10 +298,16 @@
         jax.ShapeDtypeStruct((qw,), F32),
         jax.ShapeDtypeStruct((kw,), F32),
     )
-    outs = pl.pallas_call(
-        functools.partial(kernel, n_grp, n_dp, rows_per),
-        name="replay",
-        out_shape=shapes,
+    v = jax.ShapeDtypeStruct
+    side = GROUP * slots
+    staged = (
+        v((KVH, side, HD), BF16), v((KVH, side, HD), BF16), v((slots, kw), BF16),
+        v((KVH, slots, side), F32), v((KVH, slots, side), F32), v((KVH, n_grp, own_rows, 2 * HD), BF16),
+    )
+    held = pl.pallas_call(
+        functools.partial(prepare, n_grp),
+        name="prepare",
+        out_shape=staged,
         in_specs=[pl.BlockSpec(memory_space=pltpu.SMEM)] + [hbm] * 6,
         out_specs=(vmem,) * 6,
         scratch_shapes=[
@@ -271,28 +317,34 @@
             pltpu.VMEM((slots, qw), BF16),
             pltpu.VMEM((slots, qw), BF16),
             pltpu.VMEM((slots, kw), BF16),
-            pltpu.VMEM((KVH, GROUP * slots, HD), BF16),
-            pltpu.VMEM((KVH, GROUP * slots, HD), BF16),
-            pltpu.VMEM((slots, kw), BF16),
-            pltpu.VMEM((KVH, slots, GROUP * slots), F32),
-            pltpu.VMEM((KVH, slots, GROUP * slots), F32),
+            dma(4 + 2 * KVH), dma(KVH, n_grp - 1), dma(KVH, n_grp),
+        ],
+        compiler_params=pltpu.CompilerParams(
+            collective_id=1, has_side_effects=True, vmem_limit_bytes=16 * 1024 * 1024
+        ),
+    )(lengths, *(pltpu.with_memory_space_constraint(x, pltpu.HBM) for x in (query[0], resp_kv[0], prefix_kv[0], query_bias, kv_bias, out_grad[0])))
+    outs = pl.pallas_call(
+        functools.partial(kernel, n_grp, n_dp, rows_per),
+        name="replay",
+        out_shape=shapes,
+        in_specs=[pl.BlockSpec(memory_space=pltpu.SMEM)] + [vmem] * 6,
+        out_specs=(vmem,) * 6,
+        scratch_shapes=[
             pltpu.VMEM((KVH, pre_rows + slots, GROUP * slots), BF16),
-            pltpu.VMEM((KVH, n_grp, own_rows, 2 * HD), BF16),
             pltpu.VMEM((KVH, n_grp, own_rows, 2 * HD), BF16),
             pltpu.VMEM((KVH, n_grp, own_rows, 2 * HD), BF16),
             pltpu.VMEM((n_grp, tile, HD), F32),
             pltpu.VMEM((n_grp, tile, HD), F32),
             pltpu.VMEM((n_dp, tile, HD), F32),
             pltpu.VMEM((n_grp, tile, HD), F32),
-            dma(4 + 2 * KVH),
-            dma(KVH, n_grp - 1), dma(KVH, n_grp), dma(KVH, n_grp - 1), dma(KVH, n_grp),
+            dma(KVH, n_grp - 1), dma(KVH, n_grp),
             dma(n_grp - 1), dma(n_grp), dma(n_dp - 1), dma(n_dp),
             dma(n_grp - 1), dma(n_grp),
         ],
         compiler_params=pltpu.CompilerParams(
             collective_id=0, has_side_effects=True, vmem_limit_bytes=24 * 1024 * 1024
         ),
-    )(lengths, *(pltpu.with_memory_space_constraint(x, pltpu.HBM) for x in (query[0], resp_kv[0], prefix_kv[0], query_bias, kv_bias, out_grad[0])))
+    )(lengths, *held)
     att, dq, dkv, dpre, qsum, kvsum = pl.pallas_call(
         write_out,
         name="write_out",

time: 23.7 us -> 24.1 us (1.017)
  Pallas kernels: 22.3 us -> 22.7 us
    pallas_call x0 -> x1, Pallas kernels: none -> 6.96 us  [local(): pl.pallas_call(functools.partial(prepare, n_grp), name='prepare', out_sha...]
    pallas_call x1, Pallas kernels: 21.1 us -> 14.5 us  [local(): pl.pallas_call(functools.partial(kernel, n_grp, n_dp, rows_per), name='re...]
where the time goes in v4:
time: 24.1 us; the launch traced here: 24 us
  Pallas kernels  22.7 us (94%)
  between operations  1.3 us (5%)
    pallas_call x1, Pallas kernels, local(): pl.pallas_call(functools.partial(kernel, n_grp, n_dp, rows_per), name='re...  14.5 us
    pallas_call x1, Pallas kernels, local(): pl.pallas_call(functools.partial(prepare, n_grp), name='prepare', out_sha...  6.96 us
    pallas_call x1, Pallas kernels, local(): pl.pallas_call(write_out, name='write_out', out_shape=shapes, in_specs=[v...  1.2 us

profile of v4, /device:TPU:0, one launch (start us, length us, event | category | flops | bytes accessed | tf_op | source)
XLA Modules:
  0.0 24.0 jit_solution(12948142152269143168)
XLA Ops:
  1.3 7.0 %prepare.1 = (bf16[4,640,128]{2,1,0:T(8,128)(2,1)S(1)}, bf16[4,640,128]{2,1,0:T(8,128)(2,1)S(1)}, bf16[128,1024]{1,0:T(8,128)(2,1)S(1)}, f32[4,128,640]{2,1,0:T(...) custom-call(s32[1,1]{1,0:T(1,128)S(6)} %copy.13.len_ref, bf16[128,2560]{1,0:T(8,128)(2,1)} %bitcast.8, ...), custom_call_target="tpu_custom_call" | custom-call | tf_op jit(solution)/shard_map/prepare/pallas_call | solution.py:307
  8.2 14.5 %replay.1 = (bf16[128,2560]{1,0:T(8,128)(2,1)S(1)}, bf16[128,2560]{1,0:T(8,128)(2,1)S(1)}, bf16[128,1024]{1,0:T(8,128)(2,1)S(1)}, bf16[16,1024]{1,0:T(8,128)(2,1...) custom-call(s32[1,1]{1,0:T(1,128)S(6)} %copy.13.len_ref, bf16[4,640,128]{2,1,0:T(8,128)(2,1)S(1)} %get-tuple-element.24.q2, ...), custom_call_target="tpu_custom_call" | custom-call | tf_op jit(solution)/shard_map/replay/pallas_call | solution.py:326
  22.8 1.2 %write_out.1 = (bf16[128,2560]{1,0:T(8,128)(2,1)}, bf16[128,2560]{1,0:T(8,128)(2,1)}, bf16[128,1024]{1,0:T(8,128)(2,1)}, bf16[16,1024]{1,0:T(8,128)(2,1)}, f32[2560]{0:T(1024)}, /*index=5*/f32[1024]{0:T(1024)}) custom-call(bf16[128,2560]{1,0:T(8,128)(2,1)S(1)} %get-tuple-element.30.refs_0_, bf16[128,2560]{1,0:T(8,128)(2,1)S(1)} %get-tuple-element.31.refs_1_, ...), custom_call_target="tpu_custom_call" | custom-call | tf_op jit(solution)/shard_map/write_out/pallas_call | solution.py:348
